TPU v7x, 128 devices: a whole 4x4x4 slice. The times are simulated.
128 devices in a mesh: dp: 8 (over x, core), mp: 16 (over z, y).
Axes of the slice: x: 4, y: 4, z: 4, core: 2. Of those that a mesh axis runs over, the one named last changes fastest.
Arguments:
- canvas: bfloat16 [16, 16, 16, 1408], P('dp'), may hold values from -6 to 6
- target: bfloat16 [16, 16, 16, 1408], P('dp'), may hold values from -6 to 6
- kernel: float32 [49, 1408], replicated, may hold values from -0.875 to 0.875
- kernel_bias: float32 [1408], replicated, may hold values from -3 to 3
- norm_gain: float32 [1408], replicated, may hold values from 0.5 to 1.5
- norm_bias: float32 [1408], replicated, may hold values from -2 to 2
- in_weight: bfloat16 [5632, 1408], P('mp'), may hold values from -0.15625 to 0.15625
- in_bias: float32 [5632], P('mp'), may hold values from -3 to 3
- out_weight: bfloat16 [5632, 1408], P('mp'), may hold values from -0.078125 to 0.078125
- out_bias: float32 [1408], replicated, may hold values from -3 to 3
- probe_vector: float32 [49, 1408], P(None, 'mp'), may hold values from -6 to 6
- shapes: int32 [16, 2], P('dp'), may hold values from 2 to 16, as said below
- send_slots: int32 [16, 16, 16], P('dp'), may hold values from -1 to 447, as said below
Outputs:
- krylov_vector: float32 [49, 1408], P(None, 'mp')
- first_rayleigh: float32 [1], replicated
- lanczos_terms: float32 [3], replicated
Inputs may be any that keep to these rules, and one draw needn't show every extreme that they name: `shapes`: one of an image's two sides equals 16. `send_slots`: A cell's entry is -1 exactly where it lies outside its image; otherwise it is d * 56 + k: the cell goes to slot k of the owner with dp index d. No two cells of one dp index share an entry, so none sends more than 56 cells to one owner; every owner receives exactly 256 cells over all dp indices; some dp index sends 56 cells to every owner.
All inputs are finite; a program needn't handle non-finite values.
Results may differ from a plain program's by a relative error of at most 0.025.
Values may be sent and summed in bfloat16 or wider, within the bound.
A program may use at most 128 MiB of HBM per device.

v0:
```python
import jax
import jax.numpy as jnp
from jax import lax
from jax.sharding import PartitionSpec as P

C = 1408
KS = 7
SIDE = 16
MOST_SRC = 448
OWN = 256
layer_eps = 1e-06
vector_eps = 1e-06
half_root = 0.7071067811865476
density_scale = 0.3989422804014327


def phi_density(values):
    return density_scale * jnp.exp(-0.5 * values * values)


def gelu_value(values):
    return 0.5 * values * (1.0 + jax.scipy.special.erf(values * half_root))


def gelu_slope(values):
    return 0.5 * (1.0 + jax.scipy.special.erf(values * half_root)) + values * phi_density(values)


def gelu_bend(values):
    return phi_density(values) * (2.0 - values * values)


def inside_mask(shapes):
    cell_axis = jnp.arange(SIDE, dtype=jnp.int32)
    tall = cell_axis[None, :, None] < shapes[:, 0][:, None, None]
    wide = cell_axis[None, None, :] < shapes[:, 1][:, None, None]
    return (tall & wide).astype(jnp.float32)


def depthwise(canvas_values, tap_weights):
    margin_cells = KS // 2
    padded = jnp.pad(
        canvas_values, ((0, 0), (margin_cells, margin_cells), (margin_cells, margin_cells), (0, 0))
    )
    running = jnp.zeros(canvas_values.shape, jnp.float32)
    for tap_row in range(KS):
        for tap_col in range(KS):
            running = (
                running
                + padded[:, tap_row : tap_row + SIDE, tap_col : tap_col + SIDE, :]
                * tap_weights[tap_row * KS + tap_col]
            )
    return running


def correlate(masked, grads):
    margin_cells = KS // 2
    padded = jnp.pad(
        masked, ((0, 0), (margin_cells, margin_cells), (margin_cells, margin_cells), (0, 0))
    )
    pieces = []
    for tap_row in range(KS):
        for tap_col in range(KS):
            window = padded[:, tap_row : tap_row + SIDE, tap_col : tap_col + SIDE, :]
            pieces.append(
                jnp.einsum("npqc,npqc->c", window, grads, preferred_element_type=jnp.float32)
            )
    return jnp.stack(pieces, 0)


def normalize(rows):
    values = rows.astype(jnp.float32)
    row_mean = jnp.mean(values, 1, keepdims=True)
    centered = values - row_mean
    deviation = jnp.sqrt(jnp.mean(centered * centered, 1, keepdims=True) + layer_eps)
    return (centered / deviation, deviation)


def model_sum(partial_value):
    return lax.psum(partial_value.astype(jnp.bfloat16), "mp").astype(jnp.float32)


def input_share(partial_value):
    return lax.psum_scatter(
        partial_value.astype(jnp.bfloat16), "mp", scatter_dimension=1, tiled=True
    ).astype(jnp.float32)


def row_stats(first_sum, second_sum):
    return lax.psum((first_sum, second_sum), "mp")


def inner_model(first_vec, second_vec):
    return lax.psum(jnp.sum(first_vec * second_vec), "mp")


def alpha_of(product, direction):
    return inner_model(product, direction)


def per_device(
    canvas,
    target,
    kernel,
    kernel_bias,
    norm_gain,
    norm_bias,
    in_weight,
    in_bias,
    out_weight,
    out_bias,
    probe_vector,
    shapes,
    send_slots,
):
    sources = lax.axis_size("dp")
    models = lax.axis_size("mp")
    model_index = lax.axis_index("mp")
    images = canvas.shape[0]
    cell_count = images * SIDE * SIDE
    shard_width = C // models
    capacity = MOST_SRC // sources
    slot_count = sources * capacity
    tokens = OWN * sources
    channel_start = model_index * shard_width
    inside = inside_mask(shapes)
    masked = canvas * inside[..., None].astype(jnp.bfloat16)
    masked_part = lax.dynamic_slice_in_dim(masked, channel_start, shard_width, 3)
    flat_slots = send_slots.reshape(cell_count)
    slot_hits = flat_slots[None, :] == jnp.arange(slot_count, dtype=jnp.int32)[:, None]
    source_cell = jnp.sum(
        jnp.where(slot_hits, jnp.arange(cell_count, dtype=jnp.int32)[None, :], 0), axis=1
    )
    slot_flags = jnp.any(slot_hits, axis=1).astype(jnp.bfloat16).reshape(sources, capacity)

    def pack_slots(values):
        return jnp.take(values, source_cell, axis=0).reshape(sources, capacity, values.shape[1])

    conv_source = masked.astype(jnp.float32)
    conved = (depthwise(conv_source, kernel) + kernel_bias).astype(jnp.bfloat16)
    diff = (target.astype(jnp.float32) - canvas.astype(jnp.float32)).astype(jnp.bfloat16)
    payload = jnp.stack([conved.reshape(cell_count, C), diff.reshape(cell_count, C)], 1).reshape(
        cell_count, 2 * C
    )
    arrived_rows, arrived_flags = (
        lax.all_to_all(pack_slots(payload), "dp", split_axis=0, concat_axis=0, tiled=True),
        lax.all_to_all(slot_flags, "dp", split_axis=0, concat_axis=0, tiled=True),
    )
    gather_live_slots = arrived_flags.reshape(slot_count) > 0.5
    live_count = gather_live_slots.astype(jnp.int32)
    gather_position = jnp.cumsum(live_count) - live_count
    row_marks = gather_live_slots[None, :] & (
        gather_position[None, :] == jnp.arange(OWN, dtype=jnp.int32)[:, None]
    )
    gather_slot_of_row = jnp.sum(
        jnp.where(row_marks, jnp.arange(slot_count, dtype=jnp.int32)[None, :], 0), axis=1
    )
    owned_rows = jnp.take(
        arrived_rows.reshape(slot_count, 2 * C), gather_slot_of_row, axis=0
    ).reshape(OWN, 2, C)
    conv_rows = owned_rows[:, 0]
    diff_rows = owned_rows[:, 1]
    normed, deviation = normalize(conv_rows)
    features = (normed * norm_gain + norm_bias).astype(jnp.bfloat16)
    pre_act = (
        jnp.einsum("tc,hc->th", features, in_weight, preferred_element_type=jnp.float32) + in_bias
    )
    activation = gelu_value(pre_act).astype(jnp.bfloat16)
    outputs = (
        model_sum(jnp.dot(activation, out_weight, preferred_element_type=jnp.float32)) + out_bias
    )
    residue = (outputs - diff_rows.astype(jnp.float32)).astype(jnp.bfloat16)
    back_act = jnp.einsum("tc,hc->th", residue, out_weight, preferred_element_type=jnp.float32)
    slope = gelu_slope(pre_act)
    curvature = back_act * gelu_bend(pre_act)
    back_pre = (back_act * slope).astype(jnp.bfloat16)
    back_feat = input_share(jnp.dot(back_pre, in_weight, preferred_element_type=jnp.float32))
    gain_part = lax.dynamic_slice_in_dim(norm_gain, channel_start, shard_width, 0)
    normed_part = lax.dynamic_slice_in_dim(normed, channel_start, shard_width, 1)
    grad_scaled = back_feat * gain_part
    grad_total, grad_cross = row_stats(
        jnp.sum(grad_scaled, 1), jnp.sum(grad_scaled * normed_part, 1)
    )
    grad_mean = grad_total[:, None] / C
    grad_corr = grad_cross[:, None] / C
    back_conv = (grad_scaled - grad_mean - normed_part * grad_corr) / deviation
    safe_slots = jnp.maximum(flat_slots, 0)

    def hessian(direction):
        full_direction = lax.all_gather(direction, "mp", axis=1, tiled=True)
        tangent = depthwise(conv_source, full_direction).astype(jnp.bfloat16).reshape(cell_count, C)
        arrived_tan = lax.all_to_all(
            pack_slots(tangent), "dp", split_axis=0, concat_axis=0, tiled=True
        )
        tan_rows = jnp.take(arrived_tan.reshape(slot_count, C), gather_slot_of_row, axis=0)
        tangent_vals = tan_rows.astype(jnp.float32)
        lift = jnp.mean(normed * tangent_vals, 1, keepdims=True)
        tan_hat = (
            tangent_vals - jnp.mean(tangent_vals, 1, keepdims=True) - normed * lift
        ) / deviation
        rate = lift / deviation
        tan_feat = (tan_hat * norm_gain).astype(jnp.bfloat16)
        tan_pre = jnp.einsum("tc,hc->th", tan_feat, in_weight, preferred_element_type=jnp.float32)
        tan_act = (slope * tan_pre).astype(jnp.bfloat16)
        tan_out = model_sum(
            jnp.dot(tan_act, out_weight, preferred_element_type=jnp.float32)
        ).astype(jnp.bfloat16)
        tan_back_act = jnp.einsum(
            "tc,hc->th", tan_out, out_weight, preferred_element_type=jnp.float32
        )
        tan_back_pre = (tan_back_act * slope + curvature * tan_pre).astype(jnp.bfloat16)
        tan_scaled = (
            input_share(jnp.dot(tan_back_pre, in_weight, preferred_element_type=jnp.float32))
            * gain_part
        )
        tan_hat_part = lax.dynamic_slice_in_dim(tan_hat, channel_start, shard_width, 1)
        tan_total, tan_cross = row_stats(
            jnp.sum(tan_scaled, 1),
            jnp.sum(tan_scaled * normed_part + grad_scaled * tan_hat_part, 1),
        )
        tan_mean = tan_total[:, None] / C
        tan_corr = tan_cross[:, None] / C
        tan_back = (
            (tan_scaled - tan_mean - tan_hat_part * grad_corr - normed_part * tan_corr) / deviation
            - back_conv * rate
        ).astype(jnp.bfloat16)
        at_slots = jnp.take(tan_back, gather_position, axis=0)
        at_slots = jnp.where(gather_live_slots[:, None], at_slots, jnp.zeros_like(at_slots))
        returned = lax.all_to_all(
            at_slots.reshape(sources, capacity, shard_width),
            "dp",
            split_axis=0,
            concat_axis=0,
            tiled=True,
        )
        cell_values = jnp.take(returned.reshape(slot_count, shard_width), safe_slots, axis=0)
        cell_values = jnp.where(flat_slots[:, None] >= 0, cell_values, jnp.zeros_like(cell_values))
        local_term = correlate(
            masked_part, cell_values.reshape(images, SIDE, SIDE, shard_width)
        ) * (1.0 / tokens)
        return (lax.psum(local_term, "dp"), local_term)

    probe_norm = jnp.sqrt(inner_model(probe_vector, probe_vector) + vector_eps)
    lanczos_one = probe_vector / probe_norm
    product_one, local_one = hessian(lanczos_one)
    alpha_one = alpha_of(product_one, lanczos_one)
    remainder_one = product_one - alpha_one * lanczos_one
    beta_one = jnp.sqrt(inner_model(remainder_one, remainder_one) + vector_eps)
    lanczos_two = remainder_one / beta_one
    product_two, local_two = hessian(lanczos_two)
    alpha_two = alpha_of(product_two, lanczos_two)
    remainder_two = product_two - alpha_two * lanczos_two - beta_one * lanczos_one
    beta_two = jnp.sqrt(inner_model(remainder_two, remainder_two) + vector_eps)
    return (
        remainder_two / beta_two,
        jnp.stack([alpha_one]),
        jnp.stack([alpha_two, beta_one, beta_two]),
    )


def solution(mesh):
    placed = (
        P("dp", None, None, None),
        P("dp", None, None, None),
        P(),
        P(),
        P(),
        P(),
        P("mp", None),
        P("mp"),
        P("mp", None),
        P(),
        P(None, "mp"),
        P("dp", None),
        P("dp", None, None),
    )
    return jax.shard_map(
        per_device, mesh=mesh, in_specs=placed, out_specs=(P(None, "mp"), P(), P()), check_vma=False
    )
```

profile of v0, /device:TPU:0, one launch (start us, length us, event | category | flops | bytes accessed | tf_op | source)
XLA Modules:
  0.0 1089.0 jit_solution(18031086385054804951)
XLA Ops:
  9.0 4.4 all-to-all-start
  13.4 1.9 slice_reduce_fusion.146
  15.3 1.8 slice_reduce_fusion.145
  20.0 42.6 %psum.112 = f32[]{:T(128)} all-reduce(f32[]{:T(128)} %multiply_reduce_fusion.5), channel_id=1, replica_groups=mesh['dp'=8,'mp'=16] {'mp'}, use_global_device_ids=true, to_apply=%region_8.9 | all-reduce | flops 1 | bytes 8 | tf_op jit(solution)/shard_map/psum | solution.py:94
  64.0 21.0 %all-gather = f32[16,88,49]{1,2,0:T(8,128)S(1)} all-gather(f32[1,88,49]{1,2,0:T(8,128)S(1)} %fusion.195), channel_id=1, replica_groups=mesh['dp'=8,'mp'=16] {'mp'}, dimensions={0}, use_global_device_ids=true | all-gather | bytes 293216 | tf_op jit(solution)/shard_map/all_gather | solution.py:190
  87.9 19.6 %add_convert_fusion.2 = bf16[2,16,16,1408]{3,2,1,0:T(8,128)(2,1)S(1)} fusion(bf16[2,16,16,1408]{3,2,1,0:T(8,128)(2,1)S(1)} %get-tuple-element.279, f32[2,16,16,1408]{3,2,1,0:T(8,128)S(1)} %get-tuple-element.278, f32[1408]{0:T(1024)S(1)} %copy-done.48, f32[1408]{0:T(1024)S(1)} %get-tuple-element.109, f32[1408]{0:T(1024)S(1)} %get-tuple-element.110, ...), kind=kLoop, calls=%fused_computation.160 | loop fusion | flops 72089600 | bytes 6048768 | tf_op jit(solution)/shard_map/convert_element_type | solution.py:140
  107.6 2.2 copy.51
  110.2 2.2 copy.52
  112.5 8.1 pad_maximum_fusion
  120.6 19.7 %add_convert_fusion.1 = bf16[2,16,16,1408]{3,2,1,0:T(8,128)(2,1)S(1)} fusion(bf16[2,16,16,1408]{3,2,1,0:T(8,128)(2,1)S(1)} %get-tuple-element.279, f32[2,16,16,1408]{3,2,1,0:T(8,128)S(1)} %get-tuple-element.278, f32[1408]{0:T(1024)S(1)} %get-tuple-element.112, f32[1408]{0:T(1024)S(1)} %get-tuple-element.113, f32[1408]{0:T(1024)S(1)} %get-tuple-element.114, ...), kind=kLoop, calls=%fused_computation.158 | loop fusion | flops 71368704 | bytes 6043136 | tf_op jit(solution)/shard_map/convert_element_type | solution.py:191
  140.3 2.9 gather_fusion.2
  143.2 2.6 broadcast_select_fusion.2
  145.9 3.8 copy.746
  149.7 4.8 all-to-all-start.2
  154.6 8.7 gather_fusion
  163.3 3.5 broadcast_select_fusion
  166.7 6.0 all-to-all-done.2
  173.9 3.6 all-to-all-start.1
  180.4 4.2 gather_fusion.3
  184.6 24.6 %all-to-all-done.1 = bf16[8,56,2816]{2,1,0:T(8,128)(2,1)S(1)} async-done(((bf16[8,56,2816]{2,1,0:T(8,128)(2,1)}), bf16[8,56,2816]{2,1,0:T(8,128)(2,1)S(1)}, u32[]{:S(2)}, u32[]{:S(2)}) %all-to-all-start.1) | async-done | bytes 2523168 | tf_op jit(solution)/shard_map/all_to_all | solution.py:146
  209.2 2.6 gather_fusion.1
  211.8 2.1 copy.53
  224.8 86.0 %all-reduce.14.cloned.1.call-done = (bf16[256,1408]{1,0:T(8,128)(2,1)}, bf16[256,1408]{1,0:T(8,128)(2,1)}) async-done(((bf16[256,1408]{1,0:T(8,128)(2,1)}, bf16[256,1408]{1,0:T(8,128)(2,1)}), (bf16[256,1408]{1,0:T(8,128)(2,1)}, bf16[256,1408]{1,0:T(8,128)(2,1)})) %all-reduce.14.cloned.1.call-update) | async-done | bytes 1441808 | tf_op jit(solution)/shard_map/psum | solution.py:80
  315.0 3.7 convolution_convert_fusion.3
  319.9 67.5 %reduce-scatter.12.cloned.1.call-done = bf16[256,88]{0,1:T(8,128)(2,1)} async-done(((bf16[256,1408]{0,1:T(8,128)(2,1)}), bf16[256,88]{0,1:T(8,128)(2,1)}) %reduce-scatter.12.cloned.1.call-update) | async-done | bytes 45072
  388.4 74.6 %reduce-scatter.10.cloned.1.call-done = bf16[256,88]{0,1:T(8,128)(2,1)} async-done(((bf16[256,1408]{0,1:T(8,128)(2,1)}), bf16[256,88]{0,1:T(8,128)(2,1)}) %reduce-scatter.10.cloned.1.call-update) | async-done | bytes 45072
  465.3 38.1 %all-reduce.7 = (f32[256]{0:T(256)S(1)}, f32[256]{0:T(256)S(1)}, f32[256]{0:T(256)S(1)}, f32[256]{0:T(256)S(1)}) all-reduce(f32[256]{0:T(256)S(1)} %get-tuple-element.261, f32[256]{0:T(256)S(1)} %get-tuple-element.8, f32[256]{0:T(256)S(1)} %get-tuple-element.6, f32[256]{0:T(256)S(1)} %get-tuple-element.258), channel_id=1, replica_groups=mesh['dp'=8,'mp'=16] {'mp'}, use_global_device_ids=true, to_apply=%region_22.25 | all-reduce | flops 1024 | bytes 8192 | tf_op jit(solution)/shard_map/psum | solution.py:90
  507.6 4.3 all-to-all-start.3
  512.0 5.9 all-to-all-done.3
  521.4 23.9 %psum.119 = f32[49,88]{1,0:T(8,128)S(1)} all-reduce(f32[49,88]{1,0:T(8,128)S(1)} %broadcast_multiply_fusion.2), channel_id=1, replica_groups=mesh['dp'=8,'mp'=16] {'dp'}, use_global_device_ids=true, to_apply=%region_23.28 | all-reduce | flops 4312 | bytes 34496 | tf_op jit(solution)/shard_map/psum | solution.py:241
  545.8 36.1 %psum.120 = f32[]{:T(128)} all-reduce(f32[]{:T(128)} %multiply_reduce_fusion.4), channel_id=1, replica_groups=mesh['dp'=8,'mp'=16] {'mp'}, use_global_device_ids=true, to_apply=%region_25.30 | all-reduce | flops 1 | bytes 8 | tf_op jit(solution)/shard_map/psum | solution.py:94
  583.2 38.1 %psum.121 = f32[]{:T(128)} all-reduce(f32[]{:T(128)} %multiply_reduce_fusion.3), channel_id=1, replica_groups=mesh['dp'=8,'mp'=16] {'mp'}, use_global_device_ids=true, to_apply=%region_27.32 | all-reduce | flops 1 | bytes 8 | tf_op jit(solution)/shard_map/psum | solution.py:94
  622.6 21.2 %all-gather.1 = f32[16,88,49]{1,2,0:T(8,128)S(1)} all-gather(f32[1,88,49]{1,2,0:T(8,128)S(1)} %fusion.194), channel_id=1, replica_groups=mesh['dp'=8,'mp'=16] {'mp'}, dimensions={0}, use_global_device_ids=true | all-gather | bytes 293216 | tf_op jit(solution)/shard_map/all_gather | solution.py:190
  644.9 80.7 %add_convert_fusion = bf16[2,16,16,1408]{3,2,1,0:T(8,128)(2,1)S(1)} fusion(bf16[2,16,16,1408]{3,2,1,0:T(8,128)(2,1)} %copy-done.3, f32[2,16,16,1408]{3,2,1,0:T(8,128)} %copy-done.1, f32[1408]{0:T(1024)S(1)} %get-tuple-element.14, f32[1408]{0:T(1024)S(1)} %get-tuple-element.15, f32[1408]{0:T(1024)S(1)} %get-tuple-element.16, f32[1408]{0:T(1024)S(1)} %get-tuple-element.17, ...), kind=kLoop, calls=%fused_computation.157 | loop fusion | flops 71368704 | bytes 6043136 | tf_op jit(solution)/shard_map/convert_element_type | solution.py:191
  725.6 3.0 gather_fusion.6
  730.1 20.7 %all_to_all.31 = bf16[8,56,1408]{2,1,0:T(8,128)(2,1)S(1)} all-to-all(bf16[8,56,1408]{2,1,0:T(8,128)(2,1)S(1)} %bitcast.832), channel_id=1, replica_groups=mesh['dp'=8,'mp'=16] {'dp'}, dimensions={0} | all-to-all | bytes 2523136 | tf_op jit(solution)/shard_map/all_to_all | solution.py:192
  750.8 2.4 gather_fusion.7
  753.2 1.9 convert_reduce_fusion
  755.6 1.8 fusion.8
  760.3 83.7 %all-reduce.12.cloned.1.call-done = bf16[256,1408]{1,0:T(8,128)(2,1)} async-done(((bf16[256,1408]{1,0:T(8,128)(2,1)}), bf16[256,1408]{1,0:T(8,128)(2,1)}) %all-reduce.12.cloned.1.call-update) | async-done | bytes 720912 | tf_op jit(solution)/shard_map/psum | solution.py:80
  844.0 3.9 convolution_convert_fusion
  848.0 72.4 %reduce-scatter.14.cloned.1.call-done = bf16[256,88]{0,1:T(8,128)(2,1)} async-done(((bf16[256,1408]{0,1:T(8,128)(2,1)}), bf16[256,88]{0,1:T(8,128)(2,1)}) %reduce-scatter.14.cloned.1.call-update) | async-done | bytes 45072
  922.6 38.1 %all-reduce.6 = (f32[256]{0:T(256)S(1)}, f32[256]{0:T(256)S(1)}) all-reduce(f32[256]{0:T(256)S(1)} %get-tuple-element.260, f32[256]{0:T(256)S(1)} %get-tuple-element.259), channel_id=1, replica_groups=mesh['dp'=8,'mp'=16] {'mp'}, use_global_device_ids=true, to_apply=%region_35.40 | all-reduce | flops 512 | bytes 4096 | tf_op jit(solution)/shard_map/psum | solution.py:90
  964.6 10.2 all_to_all.32
  978.3 23.9 %psum.125 = f32[49,88]{1,0:T(8,128)S(1)} all-reduce(f32[49,88]{1,0:T(8,128)S(1)} %broadcast_multiply_fusion.1), channel_id=1, replica_groups=mesh['dp'=8,'mp'=16] {'dp'}, use_global_device_ids=true, to_apply=%region_36.41 | all-reduce | flops 4312 | bytes 34496 | tf_op jit(solution)/shard_map/psum | solution.py:241
  1003.5 36.2 %psum.126 = f32[]{:T(128)} all-reduce(f32[]{:T(128)} %multiply_reduce_fusion.2), channel_id=1, replica_groups=mesh['dp'=8,'mp'=16] {'mp'}, use_global_device_ids=true, to_apply=%region_38.43 | all-reduce | flops 1 | bytes 8 | tf_op jit(solution)/shard_map/psum | solution.py:94
  1039.6 2.0 multiply_reduce_fusion.1
  1041.6 38.1 %psum.127 = f32[]{:T(128)} all-reduce(f32[]{:T(128)} %get-tuple-element.272), channel_id=1, replica_groups=mesh['dp'=8,'mp'=16] {'mp'}, use_global_device_ids=true, to_apply=%region_40.45 | all-reduce | flops 1 | bytes 8 | tf_op jit(solution)/shard_map/psum | solution.py:94
  (240 shorter events, 60.9 us)
Async XLA Ops:
  7.2 214.5 %copy-start = (bf16[352,1408]{1,0:T(8,128)(2,1)S(1)}, bf16[352,1408]{1,0:T(8,128)(2,1)}, u32[]{:S(2)}) copy-start(bf16[352,1408]{1,0:T(8,128)(2,1)} %param.29) | copy-start | bytes 2973700
  7.2 80.1 %copy-start.13 = (bf16[2,16,16,1408]{3,2,1,0:T(8,128)(2,1)S(1)}, bf16[2,16,16,1408]{3,2,1,0:T(8,128)(2,1)}, u32[]{:S(2)}) copy-start(bf16[2,16,16,1408]{3,2,1,0:T(8,128)(2,1)} %param.21) | copy-start | bytes 4325380
  8.1 55.9 %copy-start.24 = (s32[512]{0:T(512)}, s32[512]{0:T(512)S(1)}, u32[]{:S(2)}) copy-start(s32[512]{0:T(512)S(1)} %broadcast_in_dim_reshape.2) | copy-start | bytes 6148
  9.0 140.7 %all-to-all-start = ((bf16[8,1,56]{2,1,0:T(2,128)(2,1)}), bf16[8,1,56]{2,1,0:T(2,128)(2,1)}, u32[]{:S(2)}, u32[]{:S(2)}) async-start(bf16[8,1,56]{2,1,0:T(2,128)(2,1)} %reshape.856), calls=%async_computation | async-start | bytes 8192 | tf_op jit(solution)/shard_map/all_to_all | solution.py:147
  86.1 57.1 %copy-start.55 = (pred[448]{0:T(512)(128)(4,1)}, pred[448]{0:T(512)(128)(4,1)S(1)}, u32[]{:S(2)}) copy-start(pred[448]{0:T(512)(128)(4,1)S(1)} %compare_and_fusion.2) | copy-start | bytes 1348
  87.6 33.0 %copy-start.1 = (f32[2,16,16,1408]{3,2,1,0:T(8,128)}, f32[2,16,16,1408]{3,2,1,0:T(8,128)S(1)}, u32[]{:S(2)}) copy-start(f32[2,16,16,1408]{3,2,1,0:T(8,128)S(1)} %get-tuple-element.278) | copy-start | bytes 8650756
  87.6 33.0 %copy-start.3 = (bf16[2,16,16,1408]{3,2,1,0:T(8,128)(2,1)}, bf16[2,16,16,1408]{3,2,1,0:T(8,128)(2,1)S(1)}, u32[]{:S(2)}) copy-start(bf16[2,16,16,1408]{3,2,1,0:T(8,128)(2,1)S(1)} %get-tuple-element.279) | copy-start | bytes 4325380
  112.5 27.8 %copy-start.35 = (s32[1024]{0:T(1024)}, s32[1024]{0:T(1024)S(1)}, u32[]{:S(2)}) copy-start(s32[1024]{0:T(1024)S(1)} %pad_clamp_fusion.3) | copy-start | bytes 12292
  149.7 23.1 %all-to-all-start.2 = ((bf16[8,56,1408]{2,1,0:T(8,128)(2,1)}), bf16[8,56,1408]{2,1,0:T(8,128)(2,1)S(1)}, u32[]{:S(2)}, u32[]{:S(2)}) async-start(bf16[8,56,1408]{2,1,0:T(8,128)(2,1)} %bitcast.212), calls=%async_computation.2 | async-start | bytes 2523136 | tf_op jit(solution)/shard_map/all_to_all | solution.py:192
  173.9 35.3 %all-to-all-start.1 = ((bf16[8,56,2816]{2,1,0:T(8,128)(2,1)}), bf16[8,56,2816]{2,1,0:T(8,128)(2,1)S(1)}, u32[]{:S(2)}, u32[]{:S(2)}) async-start(bf16[8,56,2816]{2,1,0:T(8,128)(2,1)} %broadcast_select_fusion), calls=%async_computation.1 | async-start | bytes 5046272 | tf_op jit(solution)/shard_map/all_to_all | solution.py:146
  177.5 133.3 %all-reduce.14.cloned.1.call-start = ((), (), s32[]{:S(2)}) async-start(), calls=%async_computation.13 | async-start | bytes 2883584 | tf_op jit(solution)/shard_map/psum | solution.py:80
  178.3 6.2 copy-start.43
  180.3 4.3 copy-start.47
  180.4 39.5 %copy-start.41 = (pred[256]{0:T(512)(128)(4,1)}, pred[256]{0:T(512)(128)(4,1)S(1)}, u32[]{:S(2)}) copy-start(pred[256]{0:T(512)(128)(4,1)S(1)} %compare_and_fusion.3) | copy-start | bytes 772
  217.1 93.7 %copy-start.4 = (bf16[256,2,1408]{2,0,1:T(8,128)(2,1)}, bf16[256,2,1408]{2,0,1:T(8,128)(2,1)S(1)}, u32[]{:S(2)}) copy-start(bf16[256,2,1408]{2,0,1:T(8,128)(2,1)S(1)} %broadcast_select_fusion.1) | copy-start | bytes 4325380
  217.3 3.7 copy-start.29
  217.6 2.8 copy-start.39
  217.6 3.3 copy-start.26
  221.7 89.1 %copy-start.58 = (f32[1408]{0:T(1024)S(1)}, f32[1408]{0:T(1024)}, u32[]{:S(2)}) copy-start(f32[1408]{0:T(1024)} %param.30) | copy-start | bytes 16900
  224.7 162.7 %reduce-scatter.12.cloned.1.call-start = ((), (), s32[]{:S(2)}) async-start(), calls=%async_computation.11 | async-start | bytes 765952
  314.8 5.0 copy-start.25
  314.9 5.0 copy-start.34
  314.9 148.1 %reduce-scatter.10.cloned.1.call-start = ((), (), s32[]{:S(2)}) async-start(), calls=%async_computation.10 | async-start | bytes 765952
  314.9 188.9 %copy-start.27 = (f32[256]{0:T(256)S(1)}, f32[256]{0:T(256)}, u32[]{:S(2)}) copy-start(f32[256]{0:T(256)} %copy-done.26) | copy-start | bytes 3076
  314.9 188.9 %copy-start.56 = (f32[256]{0:T(256)S(1)}, f32[256]{0:T(256)}, u32[]{:S(2)}) copy-start(f32[256]{0:T(256)} %get-tuple-element.285) | copy-start | bytes 3076
  315.0 191.8 %copy-start.44 = (pred[448]{0:T(512)(128)(4,1)S(1)}, pred[448]{0:T(512)(128)(4,1)}, u32[]{:S(2)}) copy-start(pred[448]{0:T(512)(128)(4,1)} %copy-done.43) | copy-start | bytes 1348
  315.0 191.8 %copy-start.50 = (pred[448]{0:T(512)(128)(4,1)S(1)}, pred[448]{0:T(512)(128)(4,1)}, u32[]{:S(2)}) copy-start(pred[448]{0:T(512)(128)(4,1)} %get-tuple-element.276) | copy-start | bytes 1348
  318.7 226.6 %copy-start.19 = (f32[49,88]{1,0:T(8,128)S(1)}, f32[49,88]{1,0:T(8,128)}, u32[]{:S(2)}) copy-start(f32[49,88]{1,0:T(8,128)} %param.31) | copy-start | bytes 51748
  318.8 184.6 %copy-start.49 = (f32[88]{0:T(128)}, f32[88]{0:T(128)S(1)}, u32[]{:S(2)}) copy-start(f32[88]{0:T(128)S(1)} %dynamic_slice.16) | copy-start | bytes 1060
  319.8 324.0 %copy-start.51 = (pred[512]{0:T(512)(128)(4,1)}, pred[512]{0:T(512)(128)(4,1)S(1)}, u32[]{:S(2)}) copy-start(pred[512]{0:T(512)(128)(4,1)S(1)} %get-tuple-element.281) | copy-start | bytes 1540
  319.9 324.0 %copy-start.53 = (pred[512]{0:T(512)(128)(4,1)}, pred[512]{0:T(512)(128)(4,1)S(1)}, u32[]{:S(2)}) copy-start(pred[512]{0:T(512)(128)(4,1)S(1)} %get-tuple-element.282) | copy-start | bytes 1540
  319.9 199.3 %copy-start.36 = (s32[1024]{0:T(1024)}, s32[1024]{0:T(1024)S(1)}, u32[]{:S(2)}) copy-start(s32[1024]{0:T(1024)S(1)} %pad_clamp_fusion.1) | copy-start | bytes 12292
  388.4 119.3 %copy-start.14 = (bf16[256,88]{1,0:T(8,128)(2,1)}, bf16[256,88]{1,0:T(8,128)(2,1)S(1)}, u32[]{:S(2)}) copy-start(bf16[256,88]{1,0:T(8,128)(2,1)S(1)} %copy.57) | copy-start | bytes 135172
  503.3 140.6 %copy-start.45 = (f32[256]{0:T(256)}, f32[256]{0:T(256)S(1)}, u32[]{:S(2)}) copy-start(f32[256]{0:T(256)S(1)} %broadcast_multiply_fusion.7) | copy-start | bytes 3076
  507.6 10.2 all-to-all-start.3
  511.9 332.1 %all-reduce.12.cloned.1.call-start = ((), (), s32[]{:S(2)}) async-start(), calls=%async_computation.9 | async-start | bytes 1441792 | tf_op jit(solution)/shard_map/psum | solution.py:80
  512.0 7.2 copy-start.37
  545.2 77.4 %copy-start.21 = (f32[49,88]{1,0:T(8,128)}, f32[49,88]{1,0:T(8,128)S(1)}, u32[]{:S(2)}) copy-start(f32[49,88]{1,0:T(8,128)S(1)} %psum.119) | copy-start | bytes 51748
  750.8 4.3 copy-start.40
  753.2 4.3 copy-start.32
  755.1 3.7 copy-start.12
  757.5 163.9 %copy-start.7 = (f32[256,1408]{1,0:T(8,128)}, f32[256,1408]{1,0:T(8,128)S(1)}, u32[]{:S(2)}) copy-start(f32[256,1408]{1,0:T(8,128)S(1)} %fusion.8) | copy-start | bytes 4325380
  760.3 160.1 %reduce-scatter.14.cloned.1.call-start = ((), (), s32[]{:S(2)}) async-start(), calls=%async_computation.12 | async-start | bytes 765952
  847.9 126.8 %copy-start.38 = (s32[1024]{0:T(1024)S(1)}, s32[1024]{0:T(1024)}, u32[]{:S(2)}) copy-start(s32[1024]{0:T(1024)} %copy-done.37) | copy-start | bytes 12292
  847.9 128.2 %copy-start.52 = (pred[512]{0:T(512)(128)(4,1)S(1)}, pred[512]{0:T(512)(128)(4,1)}, u32[]{:S(2)}) copy-start(pred[512]{0:T(512)(128)(4,1)} %copy-done.51) | copy-start | bytes 1540
  847.9 128.2 %copy-start.54 = (pred[512]{0:T(512)(128)(4,1)S(1)}, pred[512]{0:T(512)(128)(4,1)}, u32[]{:S(2)}) copy-start(pred[512]{0:T(512)(128)(4,1)} %copy-done.53) | copy-start | bytes 1540
  847.9 154.2 %copy-start.20 = (f32[49,88]{1,0:T(8,128)S(1)}, f32[49,88]{1,0:T(8,128)}, u32[]{:S(2)}) copy-start(f32[49,88]{1,0:T(8,128)} %param.31) | copy-start | bytes 51748
  847.9 154.2 %copy-start.22 = (f32[49,88]{1,0:T(8,128)S(1)}, f32[49,88]{1,0:T(8,128)}, u32[]{:S(2)}) copy-start(f32[49,88]{1,0:T(8,128)} %copy-done.21) | copy-start | bytes 51748
  (21 other events, 35.7 us)
Sparse Core Ops, SparseCore 0:
  224.8 85.8 all-reduce.13
  315.0 72.4 reduce-scatter.11
  390.7 72.2 reduce-scatter.9
  760.4 83.6 all-reduce.11
  848.1 72.2 reduce-scatter.13
where the time goes:
time: 1100 us; the launch traced here: 1090 us
  waiting for transfers between devices  421 us (38%)
  blocking collectives  388 us (35%)
  other arithmetic  169 us (15%)
  local copies, waits for them, and re-layouts  59.9 us (5%)
  starting transfers between devices  17.3 us (2%)
  between operations  17.1 us (2%)
  matrix products  17 us (2%)
    unnamed x8, waiting for transfers between devices  215 us
    psum x5, blocking collectives, inner_model(): return lax.psum(jnp.sum(first_vec * second_vec), 'mp')  191 us
    psum x2, waiting for transfers between devices, model_sum(): lax.psum(partial_value.astype(jnp.bfloat16), 'mp').astype(jnp.float32)  170 us
    convert_element_type x2, other arithmetic, hessian(): depthwise(conv_source, full_direction).astype(jnp.bfloat16)  100 us
    psum x2, blocking collectives, row_stats(): return lax.psum((first_sum, second_sum), 'mp')  76.1 us
    psum x2, blocking collectives, hessian(): return (lax.psum(local_term, 'dp'), local_term)  47.7 us
    all_gather x2, blocking collectives, hessian(): full_direction = lax.all_gather(direction, 'mp', axis=1, tiled=True)  42.2 us
    all_to_all x1, waiting for transfers between devices, per_device(): lax.all_to_all(pack_slots(payload), 'dp', split_axis=0, concat_axis=0, ti...  24.6 us
  transfers between devices with their start and end apart: 9, of which 8 were waited for; matrix products, arithmetic and copies ran while one was open for 9% of the time, Pallas kernels for 0%

commit v1 on v0

--- a/solution.py
+++ b/solution.py
@@ -187,7 +187,9 @@
     safe_slots = jnp.maximum(flat_slots, 0)
 
     def hessian(direction):
-        full_direction = lax.all_gather(direction, "mp", axis=1, tiled=True)
+        full_direction = jnp.concatenate(
+            lax.all_to_all(jnp.stack([direction] * lax.axis_size("mp")), "mp", 0, 0), axis=1
+        )
         tangent = depthwise(conv_source, full_direction).astype(jnp.bfloat16).reshape(cell_count, C)
         arrived_tan = lax.all_to_all(
             pack_slots(tangent), "dp", split_axis=0, concat_axis=0, tiled=True

time: 1100 us -> 1170 us (1.064)
  other arithmetic: 169 us -> 228 us
  local copies, waits for them, and re-layouts: 59.9 us -> 97.7 us
  blocking collectives: 388 us -> 358 us
    convert_element_type x2, other arithmetic: 100 us -> 161 us  [hessian(): depthwise(conv_source, full_direction).astype(jnp.bfloat16)]
    all_gather x2 -> x0, blocking collectives: 42.2 us -> none  [hessian(): full_direction = lax.all_gather(direction, 'mp', axis=1, tiled=True)]
    mul x0 -> x98, local copies, waits for them, and re-layouts: none -> 37.1 us  [depthwise(): padded[:, tap_row:tap_row + SIDE, tap_col:tap_col + SIDE, :]]
    all_to_all x0 -> x1, blocking collectives: none -> 12.4 us  [hessian(): lax.all_to_all(jnp.stack([direction] * lax.axis_size('mp')), 'mp', 0, 0)]
  transfers between devices with their start and end apart: 9 -> 10, of which waited for: 8 -> 8; matrix products, arithmetic and copies ran while one was open for 9% -> 14% of each run, Pallas kernels for 0% -> 0%
where the time goes in v1:
time: 1170 us; the launch traced here: 1160 us
  waiting for transfers between devices  420 us (36%)
  blocking collectives  358 us (31%)
  other arithmetic  228 us (19%)
  local copies, waits for them, and re-layouts  97.7 us (8%)
  starting transfers between devices  21.3 us (2%)
  between operations  17.5 us (1%)
  matrix products  17 us (1%)
    unnamed x8, waiting for transfers between devices  215 us
    psum x5, blocking collectives, inner_model(): return lax.psum(jnp.sum(first_vec * second_vec), 'mp')  191 us
    psum x2, waiting for transfers between devices, model_sum(): lax.psum(partial_value.astype(jnp.bfloat16), 'mp').astype(jnp.float32)  169 us
    convert_element_type x2, other arithmetic, hessian(): depthwise(conv_source, full_direction).astype(jnp.bfloat16)  161 us
    psum x2, blocking collectives, row_stats(): return lax.psum((first_sum, second_sum), 'mp')  76.1 us
    psum x2, blocking collectives, hessian(): return (lax.psum(local_term, 'dp'), local_term)  47.7 us
    mul x98, local copies, waits for them, and re-layouts, depthwise(): padded[:, tap_row:tap_row + SIDE, tap_col:tap_col + SIDE, :]  37.1 us
    all_to_all x1, waiting for transfers between devices, per_device(): lax.all_to_all(pack_slots(payload), 'dp', split_axis=0, concat_axis=0, ti...  24.8 us
  transfers between devices with their start and end apart: 10, of which 8 were waited for; matrix products, arithmetic and copies ran while one was open for 14% of the time, Pallas kernels for 0%

profile of v1, /device:TPU:0, one launch (start us, length us, event | category | flops | bytes accessed | tf_op | source)
XLA Modules:
  0.0 1160.1 jit_solution(12982487784986634606)
XLA Ops:
  8.7 42.7 %psum.112 = f32[]{:T(128)} all-reduce(f32[]{:T(128)} %multiply_reduce_fusion.5), channel_id=1, replica_groups=mesh['dp'=8,'mp'=16] {'mp'}, use_global_device_ids=true, to_apply=%region_8.9 | all-reduce | flops 1 | bytes 8 | tf_op jit(solution)/shard_map/psum | solution.py:94
  53.6 3.6 all-to-all-start.2
  57.2 1.9 slice_reduce_fusion.146
  59.1 1.8 slice_reduce_fusion.145
  65.3 19.7 %add_convert_fusion.2 = bf16[2,16,16,1408]{3,2,1,0:T(8,128)(2,1)S(1)} fusion(bf16[2,16,16,1408]{3,2,1,0:T(8,128)(2,1)S(1)} %get-tuple-element.279, f32[2,16,16,1408]{3,2,1,0:T(8,128)S(1)} %get-tuple-element.278, f32[1408]{0:T(1024)S(1)} %copy-done.48, f32[1408]{0:T(1024)S(1)} %get-tuple-element.158, f32[1408]{0:T(1024)S(1)} %get-tuple-element.159, ...), kind=kLoop, calls=%fused_computation.160 | loop fusion | flops 72089600 | bytes 6048768 | tf_op jit(solution)/shard_map/convert_element_type | solution.py:140
  85.0 2.2 copy.45
  87.5 2.2 copy.46
  89.8 8.1 pad_maximum_fusion
  98.0 4.1 copy.738
  102.7 4.3 all-to-all-start
  112.5 80.7 %add_convert_fusion.1 = bf16[2,16,16,1408]{3,2,1,0:T(8,128)(2,1)S(1)} fusion(bf16[2,16,16,1408]{3,2,1,0:T(8,128)(2,1)} %copy-done.3, f32[2,16,16,1408]{3,2,1,0:T(8,128)} %copy-done.1, f32[1408]{0:T(1024)S(1)} %mul.2012, f32[1408]{0:T(1024)S(1)} %mul.2009, f32[1408]{0:T(1024)S(1)} %mul.2006, f32[1408]{0:T(1024)S(1)} %mul.2003, f32[1408]{0:T(1024)S(1)} %mul.2000, ...), kind=kLoop, calls=%fused_computation.158 | loop fusion | flops 71368704 | bytes 6043136 | tf_op jit(solution)/shard_map/convert_element_type | solution.py:193
  193.2 2.8 gather_fusion.2
  196.1 2.5 broadcast_select_fusion.2
  198.6 4.8 all-to-all-start.3
  203.4 8.7 gather_fusion
  212.1 3.5 broadcast_select_fusion
  215.6 6.1 all-to-all-done.3
  222.7 3.6 all-to-all-start.1
  228.9 4.2 gather_fusion.3
  233.1 24.8 %all-to-all-done.1 = bf16[8,56,2816]{2,1,0:T(8,128)(2,1)S(1)} async-done(((bf16[8,56,2816]{2,1,0:T(8,128)(2,1)}), bf16[8,56,2816]{2,1,0:T(8,128)(2,1)S(1)}, u32[]{:S(2)}, u32[]{:S(2)}) %all-to-all-start.1) | async-done | bytes 2523168 | tf_op jit(solution)/shard_map/all_to_all | solution.py:146
  258.0 2.6 gather_fusion.1
  260.6 1.7 copy.47
  273.2 87.7 %all-reduce.14.cloned.1.call-done = (bf16[256,1408]{1,0:T(8,128)(2,1)}, bf16[256,1408]{1,0:T(8,128)(2,1)}) async-done(((bf16[256,1408]{1,0:T(8,128)(2,1)}, bf16[256,1408]{1,0:T(8,128)(2,1)}), (bf16[256,1408]{1,0:T(8,128)(2,1)}, bf16[256,1408]{1,0:T(8,128)(2,1)})) %all-reduce.14.cloned.1.call-update) | async-done | bytes 1441808 | tf_op jit(solution)/shard_map/psum | solution.py:80
  360.9 1.7 fusion.18
  365.1 3.7 convolution_convert_fusion.3
  370.1 67.5 %reduce-scatter.12.cloned.1.call-done = bf16[256,88]{0,1:T(8,128)(2,1)} async-done(((bf16[256,1408]{0,1:T(8,128)(2,1)}), bf16[256,88]{0,1:T(8,128)(2,1)}) %reduce-scatter.12.cloned.1.call-update) | async-done | bytes 45072
  438.5 74.6 %reduce-scatter.10.cloned.1.call-done = bf16[256,88]{0,1:T(8,128)(2,1)} async-done(((bf16[256,1408]{0,1:T(8,128)(2,1)}), bf16[256,88]{0,1:T(8,128)(2,1)}) %reduce-scatter.10.cloned.1.call-update) | async-done | bytes 45072
  515.4 38.1 %all-reduce.7 = (f32[256]{0:T(256)S(1)}, f32[256]{0:T(256)S(1)}, f32[256]{0:T(256)S(1)}, f32[256]{0:T(256)S(1)}) all-reduce(f32[256]{0:T(256)S(1)} %get-tuple-element.261, f32[256]{0:T(256)S(1)} %get-tuple-element.8, f32[256]{0:T(256)S(1)} %get-tuple-element.6, f32[256]{0:T(256)S(1)} %get-tuple-element.258), channel_id=1, replica_groups=mesh['dp'=8,'mp'=16] {'mp'}, use_global_device_ids=true, to_apply=%region_22.25 | all-reduce | flops 1024 | bytes 8192 | tf_op jit(solution)/shard_map/psum | solution.py:90
  557.8 4.3 all-to-all-start.4
  562.3 5.7 all-to-all-done.4
  571.5 23.9 %psum.119 = f32[49,88]{1,0:T(8,128)S(1)} all-reduce(f32[49,88]{1,0:T(8,128)S(1)} %broadcast_multiply_fusion.2), channel_id=1, replica_groups=mesh['dp'=8,'mp'=16] {'dp'}, use_global_device_ids=true, to_apply=%region_23.28 | all-reduce | flops 4312 | bytes 34496 | tf_op jit(solution)/shard_map/psum | solution.py:243
  596.0 36.1 %psum.120 = f32[]{:T(128)} all-reduce(f32[]{:T(128)} %multiply_reduce_fusion.4), channel_id=1, replica_groups=mesh['dp'=8,'mp'=16] {'mp'}, use_global_device_ids=true, to_apply=%region_25.30 | all-reduce | flops 1 | bytes 8 | tf_op jit(solution)/shard_map/psum | solution.py:94
  633.3 38.1 %psum.121 = f32[]{:T(128)} all-reduce(f32[]{:T(128)} %multiply_reduce_fusion.3), channel_id=1, replica_groups=mesh['dp'=8,'mp'=16] {'mp'}, use_global_device_ids=true, to_apply=%region_27.32 | all-reduce | flops 1 | bytes 8 | tf_op jit(solution)/shard_map/psum | solution.py:94
  672.9 12.4 %all_to_all.41 = f32[16,49,88]{2,1,0:T(8,128)S(1)} all-to-all(f32[16,49,88]{2,1,0:T(8,128)S(1)} %stack.408), channel_id=1, replica_groups=mesh['dp'=8,'mp'=16] {'mp'}, dimensions={0} | all-to-all | bytes 551936 | tf_op jit(solution)/shard_map/all_to_all | solution.py:191
  719.7 80.6 %add_convert_fusion = bf16[2,16,16,1408]{3,2,1,0:T(8,128)(2,1)S(1)} fusion(bf16[2,16,16,1408]{3,2,1,0:T(8,128)(2,1)} %copy-done.3, f32[2,16,16,1408]{3,2,1,0:T(8,128)} %copy-done.1, f32[1408]{0:T(1024)} %mul.2190, f32[1408]{0:T(1024)} %mul.2187, f32[1408]{0:T(1024)} %mul.2184, f32[1408]{0:T(1024)} %mul.2181, f32[1408]{0:T(1024)} %mul.2178, f32[1408]{0:T(1024)} %mul.2175, ...), kind=kLoop, calls=%fused_computation.157 | loop fusion | flops 71368704 | bytes 6043136 | tf_op jit(solution)/shard_map/convert_element_type | solution.py:193
  800.3 3.0 gather_fusion.6
  804.8 20.9 %all_to_all.42 = bf16[8,56,1408]{2,1,0:T(8,128)(2,1)S(1)} all-to-all(bf16[8,56,1408]{2,1,0:T(8,128)(2,1)S(1)} %bitcast.820), channel_id=1, replica_groups=mesh['dp'=8,'mp'=16] {'dp'}, dimensions={0} | all-to-all | bytes 2523136 | tf_op jit(solution)/shard_map/all_to_all | solution.py:194
  825.7 2.4 gather_fusion.7
  828.1 1.9 convert_reduce_fusion
  830.6 1.8 fusion.8
  835.3 81.4 %all-reduce.12.cloned.1.call-done = bf16[256,1408]{1,0:T(8,128)(2,1)} async-done(((bf16[256,1408]{1,0:T(8,128)(2,1)}), bf16[256,1408]{1,0:T(8,128)(2,1)}) %all-reduce.12.cloned.1.call-update) | async-done | bytes 720912 | tf_op jit(solution)/shard_map/psum | solution.py:80
  916.7 3.9 convolution_convert_fusion
  920.6 72.4 %reduce-scatter.14.cloned.1.call-done = bf16[256,88]{0,1:T(8,128)(2,1)} async-done(((bf16[256,1408]{0,1:T(8,128)(2,1)}), bf16[256,88]{0,1:T(8,128)(2,1)}) %reduce-scatter.14.cloned.1.call-update) | async-done | bytes 45072
  995.2 38.1 %all-reduce.6 = (f32[256]{0:T(256)S(1)}, f32[256]{0:T(256)S(1)}) all-reduce(f32[256]{0:T(256)S(1)} %get-tuple-element.260, f32[256]{0:T(256)S(1)} %get-tuple-element.259), channel_id=1, replica_groups=mesh['dp'=8,'mp'=16] {'mp'}, use_global_device_ids=true, to_apply=%region_35.40 | all-reduce | flops 512 | bytes 4096 | tf_op jit(solution)/shard_map/psum | solution.py:90
  1037.2 10.0 all_to_all.43
  1050.8 23.9 %psum.125 = f32[49,88]{1,0:T(8,128)S(1)} all-reduce(f32[49,88]{1,0:T(8,128)S(1)} %broadcast_multiply_fusion.1), channel_id=1, replica_groups=mesh['dp'=8,'mp'=16] {'dp'}, use_global_device_ids=true, to_apply=%region_36.41 | all-reduce | flops 4312 | bytes 34496 | tf_op jit(solution)/shard_map/psum | solution.py:243
  1075.3 36.2 %psum.126 = f32[]{:T(128)} all-reduce(f32[]{:T(128)} %multiply_reduce_fusion.2), channel_id=1, replica_groups=mesh['dp'=8,'mp'=16] {'mp'}, use_global_device_ids=true, to_apply=%region_38.43 | all-reduce | flops 1 | bytes 8 | tf_op jit(solution)/shard_map/psum | solution.py:94
  1112.7 38.1 %psum.127 = f32[]{:T(128)} all-reduce(f32[]{:T(128)} %get-tuple-element.272), channel_id=1, replica_groups=mesh['dp'=8,'mp'=16] {'mp'}, use_global_device_ids=true, to_apply=%region_40.45 | all-reduce | flops 1 | bytes 8 | tf_op jit(solution)/shard_map/psum | solution.py:94
  (337 shorter events, 97.9 us)
Async XLA Ops:
  7.2 262.9 %copy-start = (bf16[352,1408]{1,0:T(8,128)(2,1)S(1)}, bf16[352,1408]{1,0:T(8,128)(2,1)}, u32[]{:S(2)}) copy-start(bf16[352,1408]{1,0:T(8,128)(2,1)} %param.29) | copy-start | bytes 2973700
  7.2 57.4 %copy-start.13 = (bf16[2,16,16,1408]{3,2,1,0:T(8,128)(2,1)S(1)}, bf16[2,16,16,1408]{3,2,1,0:T(8,128)(2,1)}, u32[]{:S(2)}) copy-start(bf16[2,16,16,1408]{3,2,1,0:T(8,128)(2,1)} %param.21) | copy-start | bytes 4325380
  53.6 49.1 %all-to-all-start.2 = ((f32[16,49,88]{2,1,0:T(8,128)}), f32[16,49,88]{2,1,0:T(8,128)S(1)}, u32[]{:S(2)}, u32[]{:S(2)}) async-start(f32[16,49,88]{2,1,0:T(8,128)} %stack.357), calls=%async_computation.2 | async-start | bytes 917504 | tf_op jit(solution)/shard_map/all_to_all | solution.py:191
  63.4 132.6 %copy-start.55 = (pred[448]{0:T(512)(128)(4,1)}, pred[448]{0:T(512)(128)(4,1)S(1)}, u32[]{:S(2)}) copy-start(pred[448]{0:T(512)(128)(4,1)S(1)} %compare_and_fusion.2) | copy-start | bytes 1348
  64.9 20.0 %copy-start.1 = (f32[2,16,16,1408]{3,2,1,0:T(8,128)}, f32[2,16,16,1408]{3,2,1,0:T(8,128)S(1)}, u32[]{:S(2)}) copy-start(f32[2,16,16,1408]{3,2,1,0:T(8,128)S(1)} %get-tuple-element.278) | copy-start | bytes 8650756
  64.9 20.0 %copy-start.3 = (bf16[2,16,16,1408]{3,2,1,0:T(8,128)(2,1)}, bf16[2,16,16,1408]{3,2,1,0:T(8,128)(2,1)S(1)}, u32[]{:S(2)}) copy-start(bf16[2,16,16,1408]{3,2,1,0:T(8,128)(2,1)S(1)} %get-tuple-element.279) | copy-start | bytes 4325380
  97.9 95.3 %copy-start.35 = (s32[1024]{0:T(1024)}, s32[1024]{0:T(1024)S(1)}, u32[]{:S(2)}) copy-start(s32[1024]{0:T(1024)S(1)} %pad_clamp_fusion.3) | copy-start | bytes 12292
  102.7 95.8 %all-to-all-start = ((bf16[8,1,56]{2,1,0:T(2,128)(2,1)}), bf16[8,1,56]{2,1,0:T(2,128)(2,1)S(1)}, u32[]{:S(2)}, u32[]{:S(2)}) async-start(bf16[8,1,56]{2,1,0:T(2,128)(2,1)} %reshape.1062), calls=%async_computation | async-start | bytes 8192 | tf_op jit(solution)/shard_map/all_to_all | solution.py:147
  198.6 23.0 %all-to-all-start.3 = ((bf16[8,56,1408]{2,1,0:T(8,128)(2,1)}), bf16[8,56,1408]{2,1,0:T(8,128)(2,1)S(1)}, u32[]{:S(2)}, u32[]{:S(2)}) async-start(bf16[8,56,1408]{2,1,0:T(8,128)(2,1)} %bitcast.210), calls=%async_computation.3 | async-start | bytes 2523136 | tf_op jit(solution)/shard_map/all_to_all | solution.py:194
  222.7 35.3 %all-to-all-start.1 = ((bf16[8,56,2816]{2,1,0:T(8,128)(2,1)}), bf16[8,56,2816]{2,1,0:T(8,128)(2,1)S(1)}, u32[]{:S(2)}, u32[]{:S(2)}) async-start(bf16[8,56,2816]{2,1,0:T(8,128)(2,1)} %broadcast_select_fusion), calls=%async_computation.1 | async-start | bytes 5046272 | tf_op jit(solution)/shard_map/all_to_all | solution.py:146
  226.3 134.6 %all-reduce.14.cloned.1.call-start = ((), (), s32[]{:S(2)}) async-start(), calls=%async_computation.15 | async-start | bytes 2883584 | tf_op jit(solution)/shard_map/psum | solution.py:80
  226.9 6.2 copy-start.43
  228.9 4.3 copy-start.47
  228.9 39.3 %copy-start.41 = (pred[256]{0:T(512)(128)(4,1)}, pred[256]{0:T(512)(128)(4,1)S(1)}, u32[]{:S(2)}) copy-start(pred[256]{0:T(512)(128)(4,1)S(1)} %compare_and_fusion.3) | copy-start | bytes 772
  265.5 95.4 %copy-start.4 = (bf16[256,2,1408]{2,0,1:T(8,128)(2,1)}, bf16[256,2,1408]{2,0,1:T(8,128)(2,1)S(1)}, u32[]{:S(2)}) copy-start(bf16[256,2,1408]{2,0,1:T(8,128)(2,1)S(1)} %broadcast_select_fusion.1) | copy-start | bytes 4325380
  265.7 3.6 copy-start.29
  266.0 2.8 copy-start.39
  266.1 3.3 copy-start.26
  270.0 90.9 %copy-start.58 = (f32[1408]{0:T(1024)S(1)}, f32[1408]{0:T(1024)}, u32[]{:S(2)}) copy-start(f32[1408]{0:T(1024)} %param.30) | copy-start | bytes 16900
  273.1 164.5 %reduce-scatter.12.cloned.1.call-start = ((), (), s32[]{:S(2)}) async-start(), calls=%async_computation.13 | async-start | bytes 765952
  365.0 5.0 copy-start.25
  365.0 5.0 copy-start.34
  365.0 148.1 %reduce-scatter.10.cloned.1.call-start = ((), (), s32[]{:S(2)}) async-start(), calls=%async_computation.12 | async-start | bytes 765952
  365.1 189.0 %copy-start.27 = (f32[256]{0:T(256)S(1)}, f32[256]{0:T(256)}, u32[]{:S(2)}) copy-start(f32[256]{0:T(256)} %copy-done.26) | copy-start | bytes 3076
  365.1 189.0 %copy-start.56 = (f32[256]{0:T(256)S(1)}, f32[256]{0:T(256)}, u32[]{:S(2)}) copy-start(f32[256]{0:T(256)} %get-tuple-element.285) | copy-start | bytes 3076
  365.1 191.9 %copy-start.44 = (pred[448]{0:T(512)(128)(4,1)S(1)}, pred[448]{0:T(512)(128)(4,1)}, u32[]{:S(2)}) copy-start(pred[448]{0:T(512)(128)(4,1)} %copy-done.43) | copy-start | bytes 1348
  365.1 191.9 %copy-start.50 = (pred[448]{0:T(512)(128)(4,1)S(1)}, pred[448]{0:T(512)(128)(4,1)}, u32[]{:S(2)}) copy-start(pred[448]{0:T(512)(128)(4,1)} %get-tuple-element.276) | copy-start | bytes 1348
  368.8 226.6 %copy-start.19 = (f32[49,88]{1,0:T(8,128)S(1)}, f32[49,88]{1,0:T(8,128)}, u32[]{:S(2)}) copy-start(f32[49,88]{1,0:T(8,128)} %param.31) | copy-start | bytes 51748
  368.9 184.6 %copy-start.49 = (f32[88]{0:T(128)}, f32[88]{0:T(128)S(1)}, u32[]{:S(2)}) copy-start(f32[88]{0:T(128)S(1)} %dynamic_slice.16) | copy-start | bytes 1060
  370.0 302.9 %copy-start.51 = (pred[512]{0:T(512)(128)(4,1)}, pred[512]{0:T(512)(128)(4,1)S(1)}, u32[]{:S(2)}) copy-start(pred[512]{0:T(512)(128)(4,1)S(1)} %get-tuple-element.281) | copy-start | bytes 1540
  370.0 302.9 %copy-start.53 = (pred[512]{0:T(512)(128)(4,1)}, pred[512]{0:T(512)(128)(4,1)S(1)}, u32[]{:S(2)}) copy-start(pred[512]{0:T(512)(128)(4,1)S(1)} %get-tuple-element.282) | copy-start | bytes 1540
  370.1 198.0 %copy-start.36 = (s32[1024]{0:T(1024)}, s32[1024]{0:T(1024)S(1)}, u32[]{:S(2)}) copy-start(s32[1024]{0:T(1024)S(1)} %pad_clamp_fusion.1) | copy-start | bytes 12292
  438.5 119.3 %copy-start.14 = (bf16[256,88]{1,0:T(8,128)(2,1)}, bf16[256,88]{1,0:T(8,128)(2,1)S(1)}, u32[]{:S(2)}) copy-start(bf16[256,88]{1,0:T(8,128)(2,1)S(1)} %copy.50) | copy-start | bytes 135172
  553.5 131.8 %copy-start.45 = (f32[256]{0:T(256)}, f32[256]{0:T(256)S(1)}, u32[]{:S(2)}) copy-start(f32[256]{0:T(256)S(1)} %broadcast_multiply_fusion.7) | copy-start | bytes 3076
  557.8 10.2 all-to-all-start.4
  562.1 354.6 %all-reduce.12.cloned.1.call-start = ((), (), s32[]{:S(2)}) async-start(), calls=%async_computation.11 | async-start | bytes 1441792 | tf_op jit(solution)/shard_map/psum | solution.py:80
  562.3 122.9 %copy-start.37 = (s32[1024]{0:T(1024)}, s32[1024]{0:T(1024)S(1)}, u32[]{:S(2)}) copy-start(s32[1024]{0:T(1024)S(1)} %pad_clamp_fusion) | copy-start | bytes 12292
  672.8 46.1 %copy-start.21 = (f32[49,88]{1,0:T(8,128)}, f32[49,88]{1,0:T(8,128)S(1)}, u32[]{:S(2)}) copy-start(f32[49,88]{1,0:T(8,128)S(1)} %broadcast_divide_fusion.1) | copy-start | bytes 51748
  825.7 4.3 copy-start.40
  828.1 4.3 copy-start.32
  830.0 3.7 copy-start.12
  832.4 161.6 %copy-start.7 = (f32[256,1408]{1,0:T(8,128)}, f32[256,1408]{1,0:T(8,128)S(1)}, u32[]{:S(2)}) copy-start(f32[256,1408]{1,0:T(8,128)S(1)} %fusion.8) | copy-start | bytes 4325380
  835.2 157.9 %reduce-scatter.14.cloned.1.call-start = ((), (), s32[]{:S(2)}) async-start(), calls=%async_computation.14 | async-start | bytes 765952
  920.6 126.6 %copy-start.38 = (s32[1024]{0:T(1024)S(1)}, s32[1024]{0:T(1024)}, u32[]{:S(2)}) copy-start(s32[1024]{0:T(1024)} %copy-done.37) | copy-start | bytes 12292
  920.6 128.0 %copy-start.52 = (pred[512]{0:T(512)(128)(4,1)S(1)}, pred[512]{0:T(512)(128)(4,1)}, u32[]{:S(2)}) copy-start(pred[512]{0:T(512)(128)(4,1)} %copy-done.51) | copy-start | bytes 1540
  920.6 128.0 %copy-start.54 = (pred[512]{0:T(512)(128)(4,1)S(1)}, pred[512]{0:T(512)(128)(4,1)}, u32[]{:S(2)}) copy-start(pred[512]{0:T(512)(128)(4,1)} %copy-done.53) | copy-start | bytes 1540
  920.6 154.0 %copy-start.22 = (f32[49,88]{1,0:T(8,128)S(1)}, f32[49,88]{1,0:T(8,128)}, u32[]{:S(2)}) copy-start(f32[49,88]{1,0:T(8,128)} %copy-done.21) | copy-start | bytes 51748
  920.6 190.8 %copy-start.20 = (f32[49,88]{1,0:T(8,128)S(1)}, f32[49,88]{1,0:T(8,128)}, u32[]{:S(2)}) copy-start(f32[49,88]{1,0:T(8,128)} %param.31) | copy-start | bytes 51748
  (22 other events, 37.4 us)
Sparse Core Ops, SparseCore 0:
  273.2 87.6 all-reduce.13
  365.1 72.4 reduce-scatter.11
  440.9 72.2 reduce-scatter.9
  835.4 81.3 all-reduce.11
  920.8 72.2 reduce-scatter.13
